TPU v7x, 32 devices: a whole 2x2x4 slice. The times are simulated.
32 devices in a mesh: dp: 8 (over z, y), chan: 4 (over x, core).
Axes of the slice: x: 2, y: 2, z: 4, core: 2. Of those that a mesh axis runs over, the one named last changes fastest.
Arguments:
- inputs: bfloat16 [16, 16, 16, 512], P('dp', None, None, 'chan'), may hold values from -6 to 6
- affine: float32 [3, 2, 512], P(None, None, 'chan'), may hold values from 0.3 to 1.3
- image_sizes: int32 [16, 2], P('dp'), may hold values from 8 to 16
- labels: int32 [16, 16, 16, 7], P('dp'), may hold values from 0 to 20
- label_mask: int32 [16, 16, 16, 7], P('dp'), may hold values 0 or 1
- unit_slots: int32 [54], replicated, may hold values from 0 to 55, as said below
- conv_master: float32 [56, 256, 512], P('dp', None, 'chan'), may hold values from -0.09375 to 0.09375
- conv_first: float32 [56, 256, 512], P('dp', None, 'chan'), may hold values from -0.00390625 to 0.00390625
- conv_second: float32 [56, 256, 512], P('dp', None, 'chan'), may hold values from 2.746582e-09 to 4.3945313e-08
- head_master: float32 [7, 256, 512], P(None, 'chan'), may hold values from -0.25 to 0.25
- head_first: float32 [7, 256, 512], P(None, 'chan'), may hold values from -0.0048828125 to 0.0048828125
- head_second: float32 [7, 256, 512], P(None, 'chan'), may hold values from 4.8828124e-09 to 7.8125e-08
- join_master: float32 [7, 256, 21], P(None, 'chan'), may hold values from -4 to 4
- join_first: float32 [7, 256, 21], P(None, 'chan'), may hold values from -0.0012207031 to 0.0012207031
- join_second: float32 [7, 256, 21], P(None, 'chan'), may hold values from 3.0517577e-10 to 4.8828124e-09
- scale_master: float32 [7, 256], P(None, 'chan'), may hold values from 1 to 4
- scale_first: float32 [7, 256], P(None, 'chan'), may hold values from -0.0024414062 to 0.0024414062
- scale_second: float32 [7, 256], P(None, 'chan'), may hold values from 1.2207031e-09 to 1.953125e-08
- step_count: int32 [1], replicated, may hold values from 2 to 20
Outputs:
- loss: float32 [1], replicated
- conv_new: float32 [56, 256, 512], P('dp', None, 'chan')
- conv_first_new: float32 [56, 256, 512], P('dp', None, 'chan')
- conv_second_new: float32 [56, 256, 512], P('dp', None, 'chan')
- head_new: float32 [7, 256, 512], P(None, 'chan')
- head_first_new: float32 [7, 256, 512], P(None, 'chan')
- head_second_new: float32 [7, 256, 512], P(None, 'chan')
- join_new: float32 [7, 256, 21], P(None, 'chan')
- join_first_new: float32 [7, 256, 21], P(None, 'chan')
- join_second_new: float32 [7, 256, 21], P(None, 'chan')
- scale_new: float32 [7, 256], P(None, 'chan')
- scale_first_new: float32 [7, 256], P(None, 'chan')
- scale_second_new: float32 [7, 256], P(None, 'chan')
Inputs may be any that keep to these rules, and one draw needn't show every extreme that they name: `unit_slots`: distinct slots; slot s belongs to index s // 7 of dp, so an index holds at most 7 blocks; slot 55 is always used.
All inputs are finite; a program needn't handle non-finite values. No bound on the sum of `label_mask` on one device may be relied on, other than what follows from the above.
Results may differ from a plain program's by a relative error of at most 0.0035.
The roundings to bfloat16 on the way count: a program that leaves them out, or rounds other values in their place, can miss the bound.
Values may be sent and summed in bfloat16 or wider, within the bound.
A program may use at most 128 MiB of HBM per device.

v0:
```python
import jax
import jax.numpy as jnp
from jax import lax
from jax.sharding import PartitionSpec as P

C = 512
K = 21
TASKS = 7
LAYERS = 3
H = 16
W = 16
beta_one = 0.9
beta_two = 0.999
eps_adam = 1e-08
decay_rate = 0.01
eps_norm = 1e-06


def valid_pixels(image_sizes):
    row_ids = jnp.arange(H)[None, :, None] < image_sizes[:, 0][:, None, None]
    col_ids = jnp.arange(W)[None, None, :] < image_sizes[:, 1][:, None, None]
    return (row_ids & col_ids).astype(jnp.float32)[..., None]


def adamw(weight, gradient, moment_one, moment_two, step_rate, step_count):
    step_float = step_count[0].astype(jnp.float32)
    moment_one = beta_one * moment_one + (1.0 - beta_one) * gradient
    moment_two = beta_two * moment_two + (1.0 - beta_two) * gradient * gradient
    first_hat = moment_one / (1.0 - beta_one**step_float)
    second_hat = moment_two / (1.0 - beta_two**step_float)
    weight = weight - step_rate * (
        first_hat / (jnp.sqrt(second_hat) + eps_adam) + decay_rate * weight
    )
    return (weight, moment_one, moment_two)


def pad_image(values):
    return jnp.pad(values, ((0, 0), (1, 1), (1, 1), (0, 0)))


def gather_channels(local_part):
    return lax.all_gather(local_part, "chan", axis=3, tiled=True)


def channel_sum(partial_term):
    return lax.psum_scatter(partial_term, "chan", scatter_dimension=3, tiled=True)


def conv_forward(gathered, kernels):
    padded = pad_image(gathered)
    summed = jnp.zeros(gathered.shape[:3] + (kernels.shape[2],), jnp.float32)
    for tap_index in range(9):
        row_shift, col_shift = divmod(tap_index, 3)
        window = padded[:, row_shift : row_shift + H, col_shift : col_shift + W, :]
        summed = summed + jnp.einsum(
            "ihwc,cd->ihwd", window, kernels[tap_index], preferred_element_type=jnp.float32
        )
    return summed


def conv_backward(gathered, grad_linear, kernels, need_input):
    padded = pad_image(gathered)
    grad_padded = pad_image(grad_linear)
    weight_grads = []
    spread_sum = jnp.zeros(gathered.shape, jnp.float32)
    for tap_index in range(9):
        row_shift, col_shift = divmod(tap_index, 3)
        window = padded[:, row_shift : row_shift + H, col_shift : col_shift + W, :]
        weight_grads.append(
            jnp.einsum("ihwc,ihwd->cd", window, grad_linear, preferred_element_type=jnp.float32)
        )
        if need_input:
            back_window = grad_padded[
                :, 2 - row_shift : 2 - row_shift + H, 2 - col_shift : 2 - col_shift + W, :
            ]
            spread_sum = spread_sum + jnp.einsum(
                "ihwd,cd->ihwc", back_window, kernels[tap_index], preferred_element_type=jnp.float32
            )
    input_grad = channel_sum(spread_sum) if need_input else None
    return (jnp.stack(weight_grads), input_grad)


def per_device(
    inputs,
    affine,
    image_sizes,
    labels,
    label_mask,
    unit_slots,
    conv_master,
    conv_first,
    conv_second,
    head_master,
    head_first,
    head_second,
    join_master,
    join_first,
    join_second,
    scale_master,
    scale_first,
    scale_second,
    step_count,
):
    inside = valid_pixels(image_sizes)
    slot_count = conv_master.shape[0]
    every_slot = lax.all_gather(conv_master.astype(jnp.bfloat16), "dp", axis=0, tiled=True)
    blocks = jnp.take(every_slot, unit_slots, axis=0)
    kernels = blocks.reshape(LAYERS, 9, C, blocks.shape[2])
    head_low = head_master.astype(jnp.bfloat16)
    join_low = join_master.astype(jnp.bfloat16)
    label_keep = label_mask.astype(jnp.float32) * inside
    counts = jnp.maximum(lax.psum(jnp.sum(label_keep, axis=(0, 1, 2)), "dp"), 1.0)
    current = (inputs.astype(jnp.float32) * inside).astype(jnp.bfloat16)
    gathered_list, linear_list, local_list = ([], [], [])
    for layer_index in range(LAYERS):
        gathered = gather_channels(current)
        linear = conv_forward(gathered, kernels[layer_index])
        output = (jax.nn.relu(linear) * affine[layer_index, 0] + affine[layer_index, 1]) * inside
        gathered_list.append(gathered)
        linear_list.append(linear)
        local_list.append(current)
        current = output.astype(jnp.bfloat16)
    features = gather_channels(current)
    flat_features = features.reshape(-1, C)
    hidden = jnp.einsum("pc,tdc->ptd", flat_features, head_low, preferred_element_type=jnp.float32)
    squares = lax.psum(jnp.sum(hidden * hidden, axis=2), "chan")
    inverse = lax.rsqrt(squares + eps_norm)[:, :, None]
    normed = hidden * inverse
    scaled = (scale_master[None] * normed).astype(jnp.bfloat16)
    partial_logits = jnp.einsum(
        "ptd,tdk->ptk", scaled, join_low, preferred_element_type=jnp.float32
    )
    logits = lax.psum(partial_logits, "chan")
    largest = jnp.max(logits, axis=2, keepdims=True)
    shifted = jnp.exp(logits - largest)
    totals = jnp.sum(shifted, axis=2, keepdims=True)
    log_norm = largest[..., 0] + jnp.log(totals[..., 0])
    onehot = (labels.reshape(-1, TASKS)[:, :, None] == jnp.arange(K)[None, None, :]).astype(
        jnp.float32
    )
    picked = jnp.sum(onehot * logits, axis=2)
    pixel_weight = label_keep.reshape(-1, TASKS) / counts[None, :]
    loss_local = jnp.sum(pixel_weight * (log_norm - picked))
    grad_logits = (pixel_weight[:, :, None] * (shifted / totals - onehot)).astype(jnp.bfloat16)
    grad_scaled = jnp.einsum(
        "ptk,tdk->ptd", grad_logits, join_low, preferred_element_type=jnp.float32
    )
    join_grad = jnp.einsum("ptd,ptk->tdk", scaled, grad_logits, preferred_element_type=jnp.float32)
    scale_grad = jnp.sum(grad_scaled * normed, axis=0)
    grad_normed = grad_scaled * scale_master[None]
    along_norm = lax.psum(jnp.sum(normed * grad_normed, axis=2), "chan")[:, :, None]
    grad_hidden = ((grad_normed - normed * along_norm) * inverse).astype(jnp.bfloat16)
    head_grad = jnp.einsum(
        "ptd,pc->tdc", grad_hidden, flat_features, preferred_element_type=jnp.float32
    )
    grad_flat = jnp.einsum("ptd,tdc->pc", grad_hidden, head_low, preferred_element_type=jnp.float32)
    grad_current = channel_sum(grad_flat.reshape(features.shape))
    conv_grads = [None] * LAYERS
    for layer_index in reversed(range(LAYERS)):
        linear = linear_list[layer_index]
        scaled_back = grad_current * inside * affine[layer_index, 0]
        grad_linear = jnp.where(linear > 0, scaled_back, 0.0).astype(jnp.bfloat16)
        gathered = gathered_list[layer_index]
        conv_grads[layer_index], grad_current = conv_backward(
            gathered, grad_linear, kernels[layer_index], layer_index > 0
        )
    unit_grads = jnp.stack(conv_grads).reshape(-1, C // 2, kernels.shape[3])
    summed_all = lax.psum(unit_grads, "dp")
    slot_base = lax.axis_index("dp") * slot_count
    picking = ((slot_base + jnp.arange(slot_count))[:, None] == unit_slots[None, :]).astype(
        jnp.float32
    )
    slot_grads = jnp.einsum("su,urc->src", picking, summed_all, precision=lax.Precision.HIGHEST)
    head_total, join_total, scale_total, loss_total = lax.psum(
        (head_grad, join_grad, scale_grad, loss_local), "dp"
    )
    conv_out = adamw(conv_master, slot_grads, conv_first, conv_second, 0.01, step_count)
    head_out = adamw(head_master, head_total, head_first, head_second, 0.03, step_count)
    join_out = adamw(join_master, join_total, join_first, join_second, 0.4, step_count)
    scale_out = adamw(scale_master, scale_total, scale_first, scale_second, 0.8, step_count)
    return (loss_total.reshape(1),) + conv_out + head_out + join_out + scale_out


def solution(mesh):
    placed = (
        P("dp", None, None, "chan"),
        P(None, None, "chan"),
        P("dp", None),
        P("dp", None, None, None),
        P("dp", None, None, None),
        P(),
        P("dp", None, "chan"),
        P("dp", None, "chan"),
        P("dp", None, "chan"),
        P(None, "chan", None),
        P(None, "chan", None),
        P(None, "chan", None),
        P(None, "chan", None),
        P(None, "chan", None),
        P(None, "chan", None),
        P(None, "chan"),
        P(None, "chan"),
        P(None, "chan"),
        P(),
    )
    return jax.shard_map(
        per_device,
        mesh=mesh,
        in_specs=placed,
        out_specs=(
            P(),
            P("dp", None, "chan"),
            P("dp", None, "chan"),
            P("dp", None, "chan"),
            P(None, "chan", None),
            P(None, "chan", None),
            P(None, "chan", None),
            P(None, "chan", None),
            P(None, "chan", None),
            P(None, "chan", None),
            P(None, "chan"),
            P(None, "chan"),
            P(None, "chan"),
        ),
        check_vma=False,
    )
```

profile of v0, /device:TPU:0, one launch (start us, length us, event | category | flops | bytes accessed | tf_op | source)
XLA Modules:
  0.0 576.6 jit_solution(2468389914004056909)
XLA Ops:
  7.3 2.0 convert_element_type.77
  10.5 1.1 fusion.130
  11.5 23.7 %psum.63 = f32[7]{0:T(128)S(1)} all-reduce(f32[7]{0:T(128)S(1)} %get-tuple-element.75), channel_id=1, replica_groups=mesh['dp'=8,'chan'=4] {'dp'}, use_global_device_ids=true, to_apply=%region_1.2 | all-reduce | flops 7 | bytes 56 | tf_op jit(solution)/shard_map/psum | solution.py:112
  36.5 7.2 %all_gather.15 = bf16[2,16,16,512]{3,2,1,0:T(8,128)(2,1)S(1)} all-gather(bf16[2,16,16,128]{3,2,1,0:T(8,128)(2,1)S(1)} %multiply_convert_fusion.6), channel_id=1, replica_groups=mesh['dp'=8,'chan'=4] {'chan'}, dimensions={3}, use_global_device_ids=true | all-gather | bytes 655360 | tf_op jit(solution)/shard_map/all_gather | solution.py:42
  43.8 36.1 %all-gather.2.cloned.1.call-done = bf16[56,256,128]{2,1,0:T(8,128)(2,1)} async-done(((bf16[7,256,128]{2,1,0:T(8,128)(2,1)}), bf16[56,256,128]{2,1,0:T(8,128)(2,1)}) %all-gather.2.cloned.1.call-update) | async-done | bytes 3670032 | tf_op jit(solution)/shard_map/all_gather | solution.py:106
  79.9 4.9 gather_fusion
  84.8 2.4 broadcast_select_fusion
  91.1 7.2 %all_gather.17 = bf16[2,16,16,512]{3,2,1,0:T(8,128)(2,1)S(1)} all-gather(bf16[2,16,16,128]{3,2,1,0:T(8,128)(2,1)S(1)} %get-tuple-element.134), channel_id=1, replica_groups=mesh['dp'=8,'chan'=4] {'chan'}, dimensions={3}, use_global_device_ids=true | all-gather | bytes 655360 | tf_op jit(solution)/shard_map/all_gather | solution.py:42
  101.9 7.3 %all_gather.18 = bf16[2,16,16,512]{3,2,1,0:T(8,128)(2,1)S(1)} all-gather(bf16[2,16,16,128]{3,2,1,0:T(8,128)(2,1)S(1)} %get-tuple-element.136), channel_id=1, replica_groups=mesh['dp'=8,'chan'=4] {'chan'}, dimensions={3}, use_global_device_ids=true | all-gather | bytes 655360 | tf_op jit(solution)/shard_map/all_gather | solution.py:42
  112.8 7.3 %all_gather.19 = bf16[2,16,16,512]{3,2,1,0:T(8,128)(2,1)S(1)} all-gather(bf16[2,16,16,128]{3,2,1,0:T(8,128)(2,1)S(1)} %get-tuple-element.138), channel_id=1, replica_groups=mesh['dp'=8,'chan'=4] {'chan'}, dimensions={3}, use_global_device_ids=true | all-gather | bytes 655360 | tf_op jit(solution)/shard_map/all_gather | solution.py:42
  120.5 10.7 %psum.64 = f32[512,7]{0,1:T(8,128)S(1)} all-reduce(f32[512,7]{0,1:T(8,128)S(1)} %get-tuple-element.140), channel_id=1, replica_groups=mesh['dp'=8,'chan'=4] {'chan'}, use_global_device_ids=true, to_apply=%region_3.4 | all-reduce | flops 3584 | bytes 28672 | tf_op jit(solution)/shard_map/psum | solution.py:126
  132.5 30.9 %all-reduce.10.cloned.1.call-done = f32[512,7,21]{0,2,1:T(8,128)} async-done(((f32[512,7,21]{0,2,1:T(8,128)}), f32[512,7,21]{0,2,1:T(8,128)}) %all-reduce.10.cloned.1.call-update) | async-done | bytes 301072 | tf_op jit(solution)/shard_map/psum | solution.py:133
  164.4 1.7 fusion.59
  166.2 2.8 multiply_reduce_fusion
  169.0 10.6 %psum.67 = f32[512,7]{0,1:T(8,128)S(1)} all-reduce(f32[512,7]{0,1:T(8,128)S(1)} %get-tuple-element.53), channel_id=1, replica_groups=mesh['dp'=8,'chan'=4] {'chan'}, use_global_device_ids=true, to_apply=%region_11.12 | all-reduce | flops 3584 | bytes 28672 | tf_op jit(solution)/shard_map/psum | solution.py:151
  179.6 1.4 multiply_convert_fusion
  181.0 2.7 fusion.60
  183.8 2.3 pad_slice_fusion.16
  186.2 2.3 pad_slice_fusion
  188.5 2.3 pad_slice_fusion.8
  190.9 1.3 fusion.134
  192.2 16.6 %reduce-scatter.4.cloned.1.call-done = f32[2,16,16,128]{3,2,1,0:T(8,128)} async-done(((f32[2,16,16,512]{3,2,1,0:T(8,128)}), f32[2,16,16,128]{3,2,1,0:T(8,128)}) %reduce-scatter.4.cloned.1.call-update) | async-done | bytes 262160 | tf_op jit(solution)/shard_map/reduce_scatter | solution.py:46
  208.8 1.1 select_convert_fusion.2
  209.9 1.2 fusion.66
  211.1 1.2 convolution_add_fusion.15
  215.1 1.3 convolution_add_fusion.8
  216.5 2.1 fusion.8
  222.8 1.1 fusion.3
  223.8 1.0 fusion.2
  224.9 1.1 fusion.1
  227.0 14.3 %reduce-scatter.6.cloned.1.call-done = f32[2,16,16,128]{3,2,1,0:T(8,128)} async-done(((f32[2,16,16,512]{3,2,1,0:T(8,128)}), f32[2,16,16,128]{3,2,1,0:T(8,128)}) %reduce-scatter.6.cloned.1.call-update) | async-done | bytes 262160 | tf_op jit(solution)/shard_map/reduce_scatter | solution.py:46
  241.3 1.1 select_convert_fusion.1
  245.8 1.3 convolution_add_fusion
  251.5 1.0 fusion.13
  252.6 1.1 fusion.12
  254.8 1.0 fusion.10
  255.8 1.0 fusion.9
  256.9 15.2 %reduce-scatter.8.cloned.1.call-done = f32[2,16,16,128]{3,2,1,0:T(8,128)} async-done(((f32[2,16,16,512]{3,2,1,0:T(8,128)}), f32[2,16,16,128]{3,2,1,0:T(8,128)}) %reduce-scatter.8.cloned.1.call-update) | async-done | bytes 262160 | tf_op jit(solution)/shard_map/reduce_scatter | solution.py:46
  272.1 1.1 select_convert_fusion
  278.5 2.9 pad_maximum_fusion
  281.4 7.1 %copy.215 = f32[54,256,128]{2,0,1:T(8,128)} copy(f32[54,256,128]{2,1,0:T(8,128)S(1)} %bitcast.450) | data formatting | bytes 14155776 | tf_op jit(solution)/shard_map/reshape | solution.py:167
  290.9 41.8 %all-reduce.5 = (f32[1]{0:T(128)}, f32[7,64,21]{1,2,0:T(8,128)S(1)}, f32[7,64]{1,0:T(8,128)S(1)}) all-reduce(f32[1]{0:T(128)} %bitcast.90, f32[7,64,21]{1,2,0:T(8,128)S(1)} %fusion.69, f32[7,64]{1,0:T(8,128)S(1)} %copy-done.86), channel_id=1, replica_groups=mesh['dp'=8,'chan'=4] {'dp'}, use_global_device_ids=true, to_apply=%region_9.10 | all-reduce | flops 9857 | bytes 78856 | tf_op jit(solution)/shard_map/psum | solution.py:174
  334.1 221.9 %all-reduce.12.cloned.1.call-done = (f32[54,256,128]{2,0,1:T(8,128)}, f32[7,64,512]{2,1,0:T(8,128)}) async-done(((f32[54,256,128]{2,0,1:T(8,128)}, f32[7,64,512]{2,1,0:T(8,128)}), (f32[54,256,128]{2,0,1:T(8,128)}, f32[7,64,512]{2,1,0:T(8,128)})) %all-reduce.12.cloned.1.call-update) | async-done | bytes 7995408 | tf_op jit(solution)/shard_map/psum | solution.py:168
  556.0 7.8 %copy_subtract_fusion = (f32[7,256,128]{2,0,1:T(8,128)S(1)}, f32[7,256,128]{2,0,1:T(8,128)S(1)}, f32[7,256,128]{2,0,1:T(8,128)S(1)}) fusion(f32[7,256,128]{2,1,0:T(8,128)S(1)} %copy-done, f32[]{:T(128)} %bitcast.217, f32[]{:T(128)} %bitcast.216, f32[7,256,128]{2,1,0:T(8,128)} %param.27, f32[7,256,128]{2,1,0:T(8,128)} %param.26, ...), kind=kOutput, calls=%fused_computation.126 | convolution fusion | flops 152076672 | bytes 12583164 | tf_op jit(solution)/shard_map/su,urc->src/dot_general | solution.py:173
  563.7 1.1 copy.219
  564.8 1.1 copy.220
  565.9 1.1 copy.221
  567.5 2.0 multiply_subtract_fusion
  (288 shorter events, 41.1 us)
Async XLA Ops:
  7.2 29.1 %copy-start.92 = (s32[54]{0:T(128)S(1)}, s32[54]{0:T(128)}, u32[]{:S(2)}) copy-start(s32[54]{0:T(128)} %param.24) | copy-start | bytes 652
  7.2 29.2 %copy-start.71 = (bf16[2,16,16,128]{3,2,1,0:T(8,128)(2,1)S(1)}, bf16[2,16,16,128]{3,2,1,0:T(8,128)(2,1)}, u32[]{:S(2)}) copy-start(bf16[2,16,16,128]{3,2,1,0:T(8,128)(2,1)} %param.19) | copy-start | bytes 393220
  7.2 36.5 %copy-start.89 = (f32[3,2,128]{2,1,0:T(2,128)S(1)}, f32[3,2,128]{2,1,0:T(2,128)}, u32[]{:S(2)}) copy-start(f32[3,2,128]{2,1,0:T(2,128)} %param.20) | copy-start | bytes 9220
  7.2 72.7 %all-gather.2.cloned.1.call-start = ((), (), s32[]{:S(2)}) async-start(), calls=%async_computation.3 | async-start | bytes 4128768 | tf_op jit(solution)/shard_map/all_gather | solution.py:106
  9.3 154.1 %all-reduce.10.cloned.1.call-start = ((), (), s32[]{:S(2)}) async-start(), calls=%async_computation.4 | async-start | bytes 688128 | tf_op jit(solution)/shard_map/psum | solution.py:133
  11.5 73.2 %copy-start.41 = (f32[2,16,16,7]{2,1,0,3:T(8,128)}, f32[2,16,16,7]{2,1,0,3:T(8,128)S(1)}, u32[]{:S(2)}) copy-start(f32[2,16,16,7]{2,1,0,3:T(8,128)S(1)} %get-tuple-element.76) | copy-start | bytes 43012
  36.2 130.0 %copy-start.75 = (s32[512,7]{0,1:T(8,128)}, s32[512,7]{0,1:T(8,128)S(1)}, u32[]{:S(2)}) copy-start(s32[512,7]{0,1:T(8,128)S(1)} %eq.28) | copy-start | bytes 43012
  43.7 88.6 %copy-start.90 = (f32[7]{0:T(128)}, f32[7]{0:T(128)S(1)}, u32[]{:S(2)}) copy-start(f32[7]{0:T(128)S(1)} %broadcast_maximum_fusion) | copy-start | bytes 88
  43.8 46.3 %copy-start.81 = (f32[128]{0:T(128)}, f32[128]{0:T(128)S(1)}, u32[]{:S(2)}) copy-start(f32[128]{0:T(128)S(1)} %get-tuple-element.132) | copy-start | bytes 1540
  43.8 57.1 %copy-start.83 = (f32[128]{0:T(128)}, f32[128]{0:T(128)S(1)}, u32[]{:S(2)}) copy-start(f32[128]{0:T(128)S(1)} %get-tuple-element.130) | copy-start | bytes 1540
  43.8 68.0 %copy-start.85 = (f32[128]{0:T(128)}, f32[128]{0:T(128)S(1)}, u32[]{:S(2)}) copy-start(f32[128]{0:T(128)S(1)} %get-tuple-element.128) | copy-start | bytes 1540
  87.4 12.2 %copy-start.12 = (bf16[2,256,128]{2,1,0:T(8,128)(2,1)}, bf16[2,256,128]{2,1,0:T(8,128)(2,1)S(1)}, u32[]{:S(2)}) copy-start(bf16[2,256,128]{2,1,0:T(8,128)(2,1)S(1)} %get-tuple-element.90) | copy-start | bytes 393220
  87.4 12.5 %copy-start.10 = (bf16[2,256,128]{2,1,0:T(8,128)(2,1)}, bf16[2,256,128]{2,1,0:T(8,128)(2,1)S(1)}, u32[]{:S(2)}) copy-start(bf16[2,256,128]{2,1,0:T(8,128)(2,1)S(1)} %get-tuple-element.89) | copy-start | bytes 393220
  87.4 12.8 %copy-start.8 = (bf16[2,256,128]{2,1,0:T(8,128)(2,1)}, bf16[2,256,128]{2,1,0:T(8,128)(2,1)S(1)}, u32[]{:S(2)}) copy-start(bf16[2,256,128]{2,1,0:T(8,128)(2,1)S(1)} %get-tuple-element.88) | copy-start | bytes 393220
  87.4 13.1 %copy-start.6 = (bf16[2,256,128]{2,1,0:T(8,128)(2,1)}, bf16[2,256,128]{2,1,0:T(8,128)(2,1)S(1)}, u32[]{:S(2)}) copy-start(bf16[2,256,128]{2,1,0:T(8,128)(2,1)S(1)} %get-tuple-element.87) | copy-start | bytes 393220
  87.4 13.4 %copy-start.4 = (bf16[2,256,128]{2,1,0:T(8,128)(2,1)}, bf16[2,256,128]{2,1,0:T(8,128)(2,1)S(1)}, u32[]{:S(2)}) copy-start(bf16[2,256,128]{2,1,0:T(8,128)(2,1)S(1)} %get-tuple-element.86) | copy-start | bytes 393220
  87.4 21.7 %copy-start.37 = (bf16[2,256,128]{2,1,0:T(8,128)(2,1)}, bf16[2,256,128]{2,1,0:T(8,128)(2,1)S(1)}, u32[]{:S(2)}) copy-start(bf16[2,256,128]{2,1,0:T(8,128)(2,1)S(1)} %get-tuple-element.85) | copy-start | bytes 393220
  87.4 22.1 %copy-start.36 = (bf16[2,256,128]{2,1,0:T(8,128)(2,1)}, bf16[2,256,128]{2,1,0:T(8,128)(2,1)S(1)}, u32[]{:S(2)}) copy-start(bf16[2,256,128]{2,1,0:T(8,128)(2,1)S(1)} %get-tuple-element.84) | copy-start | bytes 393220
  87.4 22.4 %copy-start.34 = (bf16[2,256,128]{2,1,0:T(8,128)(2,1)}, bf16[2,256,128]{2,1,0:T(8,128)(2,1)S(1)}, u32[]{:S(2)}) copy-start(bf16[2,256,128]{2,1,0:T(8,128)(2,1)S(1)} %get-tuple-element.83) | copy-start | bytes 393220
  87.5 22.7 %copy-start.32 = (bf16[2,256,128]{2,1,0:T(8,128)(2,1)}, bf16[2,256,128]{2,1,0:T(8,128)(2,1)S(1)}, u32[]{:S(2)}) copy-start(bf16[2,256,128]{2,1,0:T(8,128)(2,1)S(1)} %get-tuple-element.82) | copy-start | bytes 393220
  87.5 23.0 %copy-start.30 = (bf16[2,256,128]{2,1,0:T(8,128)(2,1)}, bf16[2,256,128]{2,1,0:T(8,128)(2,1)S(1)}, u32[]{:S(2)}) copy-start(bf16[2,256,128]{2,1,0:T(8,128)(2,1)S(1)} %get-tuple-element.81) | copy-start | bytes 393220
  87.5 23.3 %copy-start.28 = (bf16[2,256,128]{2,1,0:T(8,128)(2,1)}, bf16[2,256,128]{2,1,0:T(8,128)(2,1)S(1)}, u32[]{:S(2)}) copy-start(bf16[2,256,128]{2,1,0:T(8,128)(2,1)S(1)} %get-tuple-element.80) | copy-start | bytes 393220
  87.5 23.6 %copy-start.26 = (bf16[2,256,128]{2,1,0:T(8,128)(2,1)}, bf16[2,256,128]{2,1,0:T(8,128)(2,1)S(1)}, u32[]{:S(2)}) copy-start(bf16[2,256,128]{2,1,0:T(8,128)(2,1)S(1)} %get-tuple-element.79) | copy-start | bytes 393220
  87.5 23.9 %copy-start.24 = (bf16[2,256,128]{2,1,0:T(8,128)(2,1)}, bf16[2,256,128]{2,1,0:T(8,128)(2,1)S(1)}, u32[]{:S(2)}) copy-start(bf16[2,256,128]{2,1,0:T(8,128)(2,1)S(1)} %get-tuple-element.78) | copy-start | bytes 393220
  87.5 24.3 %copy-start.22 = (bf16[2,256,128]{2,1,0:T(8,128)(2,1)}, bf16[2,256,128]{2,1,0:T(8,128)(2,1)S(1)}, u32[]{:S(2)}) copy-start(bf16[2,256,128]{2,1,0:T(8,128)(2,1)S(1)} %get-tuple-element.77) | copy-start | bytes 393220
  111.7 19.5 %copy-start.69 = (f32[7,64,21]{1,2,0:T(8,128)S(1)}, f32[7,64,21]{1,2,0:T(8,128)}, u32[]{:S(2)}) copy-start(f32[7,64,21]{1,2,0:T(8,128)} %param.31) | copy-start | bytes 112900
  111.8 19.5 %copy-start.77 = (f32[7,64]{1,0:T(8,128)S(1)}, f32[7,64]{1,0:T(8,128)}, u32[]{:S(2)}) copy-start(f32[7,64]{1,0:T(8,128)} %param.34) | copy-start | bytes 5380
  132.3 76.5 %reduce-scatter.4.cloned.1.call-start = ((), (), s32[]{:S(2)}) async-start(), calls=%async_computation.5 | async-start | bytes 1310720 | tf_op jit(solution)/shard_map/reduce_scatter | solution.py:46
  132.5 47.1 %copy-start.79 = (f32[512,7]{0,1:T(8,128)}, f32[512,7]{0,1:T(8,128)S(1)}, u32[]{:S(2)}) copy-start(f32[512,7]{0,1:T(8,128)S(1)} %broadcast_divide_fusion) | copy-start | bytes 43012
  183.7 57.6 %reduce-scatter.6.cloned.1.call-start = ((), (), s32[]{:S(2)}) async-start(), calls=%async_computation.6 | async-start | bytes 1310720 | tf_op jit(solution)/shard_map/reduce_scatter | solution.py:46
  192.2 20.2 %copy-start.35 = (bf16[2,256,128]{2,1,0:T(8,128)(2,1)S(1)}, bf16[2,256,128]{2,1,0:T(8,128)(2,1)}, u32[]{:S(2)}) copy-start(bf16[2,256,128]{2,1,0:T(8,128)(2,1)} %copy-done.34) | copy-start | bytes 393220
  216.4 55.6 %reduce-scatter.8.cloned.1.call-start = ((), (), s32[]{:S(2)}) async-start(), calls=%async_computation.7 | async-start | bytes 1310720 | tf_op jit(solution)/shard_map/reduce_scatter | solution.py:46
  225.9 15.4 %copy-start.84 = (f32[128]{0:T(128)S(1)}, f32[128]{0:T(128)}, u32[]{:S(2)}) copy-start(f32[128]{0:T(128)} %copy-done.83) | copy-start | bytes 1540
  225.9 16.5 %copy-start.21 = (bf16[2,256,128]{2,1,0:T(8,128)(2,1)S(1)}, bf16[2,256,128]{2,1,0:T(8,128)(2,1)}, u32[]{:S(2)}) copy-start(bf16[2,256,128]{2,1,0:T(8,128)(2,1)} %copy-done.20) | copy-start | bytes 393220
  225.9 16.8 %copy-start.19 = (bf16[2,256,128]{2,1,0:T(8,128)(2,1)S(1)}, bf16[2,256,128]{2,1,0:T(8,128)(2,1)}, u32[]{:S(2)}) copy-start(bf16[2,256,128]{2,1,0:T(8,128)(2,1)} %copy-done.18) | copy-start | bytes 393220
  227.0 16.1 %copy-start.17 = (bf16[2,256,128]{2,1,0:T(8,128)(2,1)S(1)}, bf16[2,256,128]{2,1,0:T(8,128)(2,1)}, u32[]{:S(2)}) copy-start(bf16[2,256,128]{2,1,0:T(8,128)(2,1)} %copy-done.16) | copy-start | bytes 393220
  247.2 308.8 %all-reduce.12.cloned.1.call-start = ((), (), s32[]{:S(2)}) async-start(), calls=%async_computation.8 | async-start | bytes 16515072 | tf_op jit(solution)/shard_map/psum | solution.py:168
  255.8 16.3 %copy-start.38 = (f32[2,16,16,128]{3,2,1,0:T(8,128)S(1)}, f32[2,16,16,128]{3,2,1,0:T(8,128)}, u32[]{:S(2)}) copy-start(f32[2,16,16,128]{3,2,1,0:T(8,128)} %get-tuple-element.135) | copy-start | bytes 786436
  255.8 16.3 %copy-start.82 = (f32[128]{0:T(128)S(1)}, f32[128]{0:T(128)}, u32[]{:S(2)}) copy-start(f32[128]{0:T(128)} %copy-done.81) | copy-start | bytes 1540
  255.8 17.4 %copy-start.53 = (bf16[2,16,16,512]{3,2,1,0:T(8,128)(2,1)S(1)}, bf16[2,16,16,512]{3,2,1,0:T(8,128)(2,1)}, u32[]{:S(2)}) copy-start(bf16[2,16,16,512]{3,2,1,0:T(8,128)(2,1)} %get-tuple-element.111) | copy-start | bytes 1572868
  256.9 16.7 %copy-start.52 = (bf16[2,16,16,512]{3,2,1,0:T(8,128)(2,1)S(1)}, bf16[2,16,16,512]{3,2,1,0:T(8,128)(2,1)}, u32[]{:S(2)}) copy-start(bf16[2,16,16,512]{3,2,1,0:T(8,128)(2,1)} %get-tuple-element.105) | copy-start | bytes 1572868
  288.6 44.1 %copy-start.87 = (f32[7,64]{1,0:T(8,128)S(1)}, f32[7,64]{1,0:T(8,128)}, u32[]{:S(2)}) copy-start(f32[7,64]{1,0:T(8,128)} %param.36) | copy-start | bytes 5380
  288.6 44.1 %copy-start.88 = (f32[7,64]{1,0:T(8,128)S(1)}, f32[7,64]{1,0:T(8,128)}, u32[]{:S(2)}) copy-start(f32[7,64]{1,0:T(8,128)} %param.35) | copy-start | bytes 5380
  288.6 44.7 %copy-start.70 = (f32[7,64,21]{1,2,0:T(8,128)S(1)}, f32[7,64,21]{1,2,0:T(8,128)}, u32[]{:S(2)}) copy-start(f32[7,64,21]{1,2,0:T(8,128)} %param.31) | copy-start | bytes 112900
  288.7 44.7 %copy-start.72 = (f32[7,64,21]{1,2,0:T(8,128)S(1)}, f32[7,64,21]{1,2,0:T(8,128)}, u32[]{:S(2)}) copy-start(f32[7,64,21]{1,2,0:T(8,128)} %param.33) | copy-start | bytes 112900
  288.7 44.7 %copy-start.73 = (f32[7,64,21]{1,2,0:T(8,128)S(1)}, f32[7,64,21]{1,2,0:T(8,128)}, u32[]{:S(2)}) copy-start(f32[7,64,21]{1,2,0:T(8,128)} %param.32) | copy-start | bytes 112900
  288.7 267.3 %copy-start = (f32[7,256,128]{2,1,0:T(8,128)S(1)}, f32[7,256,128]{2,1,0:T(8,128)}, u32[]{:S(2)}) copy-start(f32[7,256,128]{2,1,0:T(8,128)} %param.25) | copy-start | bytes 2752516
  288.7 267.3 %copy-start.93 = (s32[54]{0:T(128)S(1)}, s32[54]{0:T(128)}, u32[]{:S(2)}) copy-start(s32[54]{0:T(128)} %param.24) | copy-start | bytes 652
  (52 other events, 118.6 us)
Sparse Core Ops, SparseCore 0:
  10.8 69.0 all-gather.1
  132.5 30.8 all-reduce.9
  183.8 24.9 reduce-scatter.3
  216.6 24.7 reduce-scatter.5
  247.3 24.7 reduce-scatter.7
  288.7 267.2 all-reduce.11
where the time goes:
time: 586 us; the launch traced here: 577 us
  waiting for transfers between devices  335 us (57%)
  blocking collectives  116 us (20%)
  matrix products  58.8 us (10%)
  local copies, waits for them, and re-layouts  29.5 us (5%)
  other arithmetic  20.3 us (3%)
  between operations  16.6 us (3%)
    psum x1, waiting for transfers between devices, per_device(): summed_all = lax.psum(unit_grads, 'dp')  222 us
    reduce_scatter x3, waiting for transfers between devices, channel_sum(): lax.psum_scatter(partial_term, 'chan', scatter_dimension=3, tiled=True)  46.2 us
    psum x1, blocking collectives, per_device(): lax.psum((head_grad, join_grad, scale_grad, loss_local), 'dp')  41.8 us
    all_gather x1, waiting for transfers between devices, per_device(): lax.all_gather(conv_master.astype(jnp.bfloat16), 'dp', axis=0, tiled=True)  36.1 us
    psum x1, waiting for transfers between devices, per_device(): logits = lax.psum(partial_logits, 'chan')  30.9 us
    all_gather x4, blocking collectives, gather_channels(): return lax.all_gather(local_part, 'chan', axis=3, tiled=True)  29 us
    psum x1, blocking collectives, per_device(): lax.psum(jnp.sum(label_keep, axis=(0, 1, 2)), 'dp')  23.7 us
    dot_general x27, matrix products, conv_backward(): jnp.einsum('ihwc,ihwd->cd', window, grad_linear, preferred_element_type=j...  22.9 us
  transfers between devices with their start and end apart: 6, of which 6 were waited for; matrix products, arithmetic and copies ran while one was open for 6% of the time, Pallas kernels for 0%

commit v1 on v0

--- a/solution.py
+++ b/solution.py
@@ -14,6 +14,14 @@
 eps_adam = 1e-08
 decay_rate = 0.01
 eps_norm = 1e-06
+
+
+def add_in_pairs(x, mesh_axis):
+    devices, total = (lax.axis_size(mesh_axis), x)
+    for far in [1 << k for k in range(devices.bit_length() - 1)]:
+        swap = [(i, i ^ far) for i in range(devices)]
+        total = total + lax.ppermute(total, mesh_axis, swap)
+    return total
 
 
 def valid_pixels(image_sizes):
@@ -165,7 +173,7 @@
             gathered, grad_linear, kernels[layer_index], layer_index > 0
         )
     unit_grads = jnp.stack(conv_grads).reshape(-1, C // 2, kernels.shape[3])
-    summed_all = lax.psum(unit_grads, "dp")
+    summed_all = add_in_pairs(unit_grads, "dp")
     slot_base = lax.axis_index("dp") * slot_count
     picking = ((slot_base + jnp.arange(slot_count))[:, None] == unit_slots[None, :]).astype(
         jnp.float32

time: 586 us -> 1010 us (1.72)
  blocking collectives: 116 us -> 405 us
  waiting for transfers between devices: 335 us -> 449 us
  other arithmetic: 20.3 us -> 41.5 us
    ppermute x0 -> x3, waiting for transfers between devices: none -> 304 us  [add_in_pairs(): total = total + lax.ppermute(total, mesh_axis, swap)]
    psum x1, blocking collectives: 41.8 us -> 328 us  [per_device(): lax.psum((head_grad, join_grad, scale_grad, loss_local), 'dp')]
    psum x1, waiting for transfers between devices: 222 us -> 32.7 us  [per_device(): lax.psum((head_grad, join_grad, scale_grad, loss_local), 'dp')]
    add x0 -> x3, other arithmetic: none -> 14.5 us  [add_in_pairs(): total = total + lax.ppermute(total, mesh_axis, swap)]
  transfers between devices with their start and end apart: 6 -> 9, of which waited for: 6 -> 8; matrix products, arithmetic and copies ran while one was open for 6% -> 4% of each run, Pallas kernels for 0% -> 0%
where the time goes in v1:
time: 1010 us; the launch traced here: 1000 us
  waiting for transfers between devices  449 us (44%)
  blocking collectives  405 us (40%)
  matrix products  59.3 us (6%)
  other arithmetic  41.5 us (4%)
  local copies, waits for them, and re-layouts  27.4 us (3%)
  between operations  16.5 us (2%)
    psum x1, blocking collectives, per_device(): lax.psum((head_grad, join_grad, scale_grad, loss_local), 'dp')  328 us
    ppermute x3, waiting for transfers between devices, add_in_pairs(): total = total + lax.ppermute(total, mesh_axis, swap)  304 us
    reduce_scatter x3, waiting for transfers between devices, channel_sum(): lax.psum_scatter(partial_term, 'chan', scatter_dimension=3, tiled=True)  48.7 us
    all_gather x1, waiting for transfers between devices, per_device(): lax.all_gather(conv_master.astype(jnp.bfloat16), 'dp', axis=0, tiled=True)  33.9 us
    psum x1, waiting for transfers between devices, per_device(): lax.psum((head_grad, join_grad, scale_grad, loss_local), 'dp')  32.7 us
    psum x1, waiting for transfers between devices, per_device(): logits = lax.psum(partial_logits, 'chan')  29.6 us
    all_gather x4, blocking collectives, gather_channels(): return lax.all_gather(local_part, 'chan', axis=3, tiled=True)  29.4 us
    psum x1, blocking collectives, per_device(): lax.psum(jnp.sum(label_keep, axis=(0, 1, 2)), 'dp')  23.7 us
  transfers between devices with their start and end apart: 9, of which 8 were waited for; matrix products, arithmetic and copies ran while one was open for 4% of the time, Pallas kernels for 0%

profile of v1, /device:TPU:0, one launch (start us, length us, event | category | flops | bytes accessed | tf_op | source)
XLA Modules:
  0.0 1004.3 jit_solution(14706308550298641893)
XLA Ops:
  7.3 2.0 convert_element_type.77
  11.5 23.7 %psum.56 = f32[7]{0:T(128)S(1)} all-reduce(f32[7]{0:T(128)S(1)} %get-tuple-element.73), channel_id=1, replica_groups=mesh['dp'=8,'chan'=4] {'dp'}, use_global_device_ids=true, to_apply=%region_1.2 | all-reduce | flops 7 | bytes 56 | tf_op jit(solution)/shard_map/psum | solution.py:120
  37.7 7.2 all_gather.15
  46.0 33.9 %all-gather.2.cloned.1.call-done = bf16[56,256,128]{2,1,0:T(8,128)(2,1)} async-done(((bf16[7,256,128]{2,1,0:T(8,128)(2,1)}), bf16[56,256,128]{2,1,0:T(8,128)(2,1)}) %all-gather.2.cloned.1.call-update) | async-done | bytes 3670032 | tf_op jit(solution)/shard_map/all_gather | solution.py:114
  79.9 4.9 gather_fusion
  84.8 2.4 broadcast_select_fusion
  91.1 7.2 all_gather.17
  101.9 7.3 all_gather.18
  112.8 7.7 all_gather.19
  120.5 2.1 multiply_reduce_fusion.2
  122.6 12.0 %psum.57 = f32[512,7]{0,1:T(8,128)} all-reduce(f32[512,7]{0,1:T(8,128)} %get-tuple-element.138), channel_id=1, replica_groups=mesh['dp'=8,'chan'=4] {'chan'}, use_global_device_ids=true, to_apply=%region_3.4 | all-reduce | flops 3584 | bytes 28672 | tf_op jit(solution)/shard_map/psum | solution.py:134
  135.9 1.9 convolution_bitcast_fusion.1
  137.9 1.4 broadcast_divide_fusion
  139.3 29.6 %all-reduce.9.cloned.1.call-done = f32[512,7,21]{0,2,1:T(8,128)} async-done(((f32[512,7,21]{0,2,1:T(8,128)}), f32[512,7,21]{0,2,1:T(8,128)}) %all-reduce.9.cloned.1.call-update) | async-done | bytes 301072 | tf_op jit(solution)/shard_map/psum | solution.py:141
  168.9 1.6 reduce_max.9
  170.5 1.7 fusion.61
  172.9 3.0 multiply_reduce_fusion
  175.8 11.8 %psum.60 = f32[512,7]{0,1:T(8,128)} all-reduce(f32[512,7]{0,1:T(8,128)} %get-tuple-element.53), channel_id=1, replica_groups=mesh['dp'=8,'chan'=4] {'chan'}, use_global_device_ids=true, to_apply=%region_11.12 | all-reduce | flops 3584 | bytes 28672 | tf_op jit(solution)/shard_map/psum | solution.py:159
  187.6 1.4 multiply_convert_fusion
  189.1 1.5 fusion.62
  190.7 2.3 pad_slice_fusion.16
  193.1 2.1 pad_slice_fusion
  195.2 2.3 pad_slice_fusion.8
  197.5 18.2 %reduce-scatter.4.cloned.1.call-done = f32[2,16,16,128]{3,2,1,0:T(8,128)} async-done(((f32[2,16,16,512]{3,2,1,0:T(8,128)}), f32[2,16,16,128]{3,2,1,0:T(8,128)}) %reduce-scatter.4.cloned.1.call-update) | async-done | bytes 262160 | tf_op jit(solution)/shard_map/reduce_scatter | solution.py:54
  221.5 2.1 fusion.10
  223.6 2.1 fusion.9
  233.1 13.3 %reduce-scatter.6.cloned.1.call-done = f32[2,16,16,128]{3,2,1,0:T(8,128)} async-done(((f32[2,16,16,512]{3,2,1,0:T(8,128)}), f32[2,16,16,128]{3,2,1,0:T(8,128)}) %reduce-scatter.6.cloned.1.call-update) | async-done | bytes 262160 | tf_op jit(solution)/shard_map/reduce_scatter | solution.py:54
  252.4 1.4 fusion.19
  253.7 1.4 fusion.18
  259.9 17.2 %reduce-scatter.8.cloned.1.call-done = f32[2,16,16,128]{3,2,1,0:T(8,128)} async-done(((f32[2,16,16,512]{3,2,1,0:T(8,128)}), f32[2,16,16,128]{3,2,1,0:T(8,128)}) %reduce-scatter.8.cloned.1.call-update) | async-done | bytes 262160 | tf_op jit(solution)/shard_map/reduce_scatter | solution.py:54
  278.2 1.4 fusion.28
  284.6 2.3 pad_maximum_fusion
  286.9 1.5 collective-permute-start
  288.5 152.6 %collective-permute-done = f32[54,256,128]{2,1,0:T(8,128)} collective-permute-done((f32[54,256,128]{2,1,0:T(8,128)S(1)}, f32[54,256,128]{2,1,0:T(8,128)}, u32[]{:S(2)}, u32[]{:S(2)}) %collective-permute-start) | collective-permute-done | bytes 7077920 | tf_op jit(solution)/shard_map/ppermute | solution.py:23
  441.0 4.2 add.336
  445.2 1.6 collective-permute-start.1
  446.8 151.6 %collective-permute-done.1 = f32[54,256,128]{2,1,0:T(8,128)S(1)} collective-permute-done((f32[54,256,128]{2,1,0:T(8,128)S(1)}, f32[54,256,128]{2,1,0:T(8,128)S(1)}, u32[]{:S(2)}, u32[]{:S(2)}) %collective-permute-start.1) | collective-permute-done | bytes 7077920 | tf_op jit(solution)/shard_map/ppermute | solution.py:23
  598.4 4.0 add.337
  602.4 2.4 collective-permute-start.2
  606.1 2.4 fusion.135
  608.5 1.5 add_subtract_fusion
  610.8 1.3 multiply_reduce_fusion.3
  612.2 1.8 fusion.71
  614.0 327.7 %all-reduce.5 = (f32[1]{0:T(128)}, f32[7,64,21]{1,2,0:T(8,128)S(1)}, f32[7,64]{1,0:T(8,128)S(1)}) all-reduce(f32[1]{0:T(128)} %bitcast.90, f32[7,64,21]{1,2,0:T(8,128)} %fusion.71, f32[7,64]{1,0:T(8,128)S(1)} %copy-done.83), channel_id=1, replica_groups=mesh['dp'=8,'chan'=4] {'dp'}, use_global_device_ids=true, to_apply=%region_9.10 | all-reduce | flops 9857 | bytes 78856 | tf_op jit(solution)/shard_map/psum | solution.py:182
  943.1 32.7 %all-reduce.11.cloned.1.call-done = f32[7,64,512]{2,1,0:T(8,128)} async-done(((f32[7,64,512]{2,1,0:T(8,128)}), f32[7,64,512]{2,1,0:T(8,128)}) %all-reduce.11.cloned.1.call-update) | async-done | bytes 917520 | tf_op jit(solution)/shard_map/psum | solution.py:182
  975.8 3.5 multiply_subtract_fusion
  979.3 6.3 add.338
  985.7 8.3 copy_subtract_fusion
  (294 shorter events, 54.2 us)
Async XLA Ops:
  7.2 30.3 %copy-start.90 = (s32[54]{0:T(128)S(1)}, s32[54]{0:T(128)}, u32[]{:S(2)}) copy-start(s32[54]{0:T(128)} %param.24) | copy-start | bytes 652
  7.2 30.4 %copy-start.71 = (bf16[2,16,16,128]{3,2,1,0:T(8,128)(2,1)S(1)}, bf16[2,16,16,128]{3,2,1,0:T(8,128)(2,1)}, u32[]{:S(2)}) copy-start(bf16[2,16,16,128]{3,2,1,0:T(8,128)(2,1)} %param.19) | copy-start | bytes 393220
  7.2 38.3 %copy-start.86 = (f32[3,2,128]{2,1,0:T(2,128)S(1)}, f32[3,2,128]{2,1,0:T(2,128)}, u32[]{:S(2)}) copy-start(f32[3,2,128]{2,1,0:T(2,128)} %param.20) | copy-start | bytes 9220
  7.2 72.7 %all-gather.2.cloned.1.call-start = ((), (), s32[]{:S(2)}) async-start(), calls=%async_computation.3 | async-start | bytes 4128768 | tf_op jit(solution)/shard_map/all_gather | solution.py:114
  9.3 159.6 %all-reduce.9.cloned.1.call-start = ((), (), s32[]{:S(2)}) async-start(), calls=%async_computation.4 | async-start | bytes 688128 | tf_op jit(solution)/shard_map/psum | solution.py:141
  11.5 26.0 %copy-start.47 = (f32[2,16,16,7]{2,1,0,3:T(8,128)}, f32[2,16,16,7]{2,1,0,3:T(8,128)S(1)}, u32[]{:S(2)}) copy-start(f32[2,16,16,7]{2,1,0,3:T(8,128)S(1)} %get-tuple-element.74) | copy-start | bytes 43012
  87.3 11.6 %copy-start.20 = (bf16[2,256,128]{2,1,0:T(8,128)(2,1)}, bf16[2,256,128]{2,1,0:T(8,128)(2,1)S(1)}, u32[]{:S(2)}) copy-start(bf16[2,256,128]{2,1,0:T(8,128)(2,1)S(1)} %get-tuple-element.90) | copy-start | bytes 393220
  87.3 11.9 %copy-start.18 = (bf16[2,256,128]{2,1,0:T(8,128)(2,1)}, bf16[2,256,128]{2,1,0:T(8,128)(2,1)S(1)}, u32[]{:S(2)}) copy-start(bf16[2,256,128]{2,1,0:T(8,128)(2,1)S(1)} %get-tuple-element.89) | copy-start | bytes 393220
  87.4 12.2 %copy-start.16 = (bf16[2,256,128]{2,1,0:T(8,128)(2,1)}, bf16[2,256,128]{2,1,0:T(8,128)(2,1)S(1)}, u32[]{:S(2)}) copy-start(bf16[2,256,128]{2,1,0:T(8,128)(2,1)S(1)} %get-tuple-element.88) | copy-start | bytes 393220
  87.4 12.5 %copy-start.14 = (bf16[2,256,128]{2,1,0:T(8,128)(2,1)}, bf16[2,256,128]{2,1,0:T(8,128)(2,1)S(1)}, u32[]{:S(2)}) copy-start(bf16[2,256,128]{2,1,0:T(8,128)(2,1)S(1)} %get-tuple-element.87) | copy-start | bytes 393220
  87.4 12.8 %copy-start.12 = (bf16[2,256,128]{2,1,0:T(8,128)(2,1)}, bf16[2,256,128]{2,1,0:T(8,128)(2,1)S(1)}, u32[]{:S(2)}) copy-start(bf16[2,256,128]{2,1,0:T(8,128)(2,1)S(1)} %get-tuple-element.86) | copy-start | bytes 393220
  87.4 13.2 %copy-start.10 = (bf16[2,256,128]{2,1,0:T(8,128)(2,1)}, bf16[2,256,128]{2,1,0:T(8,128)(2,1)S(1)}, u32[]{:S(2)}) copy-start(bf16[2,256,128]{2,1,0:T(8,128)(2,1)S(1)} %get-tuple-element.85) | copy-start | bytes 393220
  87.4 21.8 %copy-start.42 = (bf16[2,256,128]{2,1,0:T(8,128)(2,1)}, bf16[2,256,128]{2,1,0:T(8,128)(2,1)S(1)}, u32[]{:S(2)}) copy-start(bf16[2,256,128]{2,1,0:T(8,128)(2,1)S(1)} %get-tuple-element.83) | copy-start | bytes 393220
  87.4 22.1 %copy-start.40 = (bf16[2,256,128]{2,1,0:T(8,128)(2,1)}, bf16[2,256,128]{2,1,0:T(8,128)(2,1)S(1)}, u32[]{:S(2)}) copy-start(bf16[2,256,128]{2,1,0:T(8,128)(2,1)S(1)} %get-tuple-element.82) | copy-start | bytes 393220
  87.4 22.4 %copy-start.38 = (bf16[2,256,128]{2,1,0:T(8,128)(2,1)}, bf16[2,256,128]{2,1,0:T(8,128)(2,1)S(1)}, u32[]{:S(2)}) copy-start(bf16[2,256,128]{2,1,0:T(8,128)(2,1)S(1)} %get-tuple-element.81) | copy-start | bytes 393220
  87.4 22.7 %copy-start.36 = (bf16[2,256,128]{2,1,0:T(8,128)(2,1)}, bf16[2,256,128]{2,1,0:T(8,128)(2,1)S(1)}, u32[]{:S(2)}) copy-start(bf16[2,256,128]{2,1,0:T(8,128)(2,1)S(1)} %get-tuple-element.80) | copy-start | bytes 393220
  87.4 23.0 %copy-start.34 = (bf16[2,256,128]{2,1,0:T(8,128)(2,1)}, bf16[2,256,128]{2,1,0:T(8,128)(2,1)S(1)}, u32[]{:S(2)}) copy-start(bf16[2,256,128]{2,1,0:T(8,128)(2,1)S(1)} %get-tuple-element.79) | copy-start | bytes 393220
  87.4 23.3 %copy-start.32 = (bf16[2,256,128]{2,1,0:T(8,128)(2,1)}, bf16[2,256,128]{2,1,0:T(8,128)(2,1)S(1)}, u32[]{:S(2)}) copy-start(bf16[2,256,128]{2,1,0:T(8,128)(2,1)S(1)} %get-tuple-element.78) | copy-start | bytes 393220
  87.5 23.6 %copy-start.30 = (bf16[2,256,128]{2,1,0:T(8,128)(2,1)}, bf16[2,256,128]{2,1,0:T(8,128)(2,1)S(1)}, u32[]{:S(2)}) copy-start(bf16[2,256,128]{2,1,0:T(8,128)(2,1)S(1)} %get-tuple-element.77) | copy-start | bytes 393220
  87.5 24.0 %copy-start.28 = (bf16[2,256,128]{2,1,0:T(8,128)(2,1)}, bf16[2,256,128]{2,1,0:T(8,128)(2,1)S(1)}, u32[]{:S(2)}) copy-start(bf16[2,256,128]{2,1,0:T(8,128)(2,1)S(1)} %get-tuple-element.76) | copy-start | bytes 393220
  87.5 24.3 %copy-start.26 = (bf16[2,256,128]{2,1,0:T(8,128)(2,1)}, bf16[2,256,128]{2,1,0:T(8,128)(2,1)S(1)}, u32[]{:S(2)}) copy-start(bf16[2,256,128]{2,1,0:T(8,128)(2,1)S(1)} %get-tuple-element.75) | copy-start | bytes 393220
  122.6 65.0 %copy-start = (f32[512,7,64]{0,2,1:T(8,128)}, f32[512,7,64]{0,2,1:T(8,128)S(1)}, u32[]{:S(2)}) copy-start(f32[512,7,64]{0,2,1:T(8,128)S(1)} %get-tuple-element.139) | copy-start | bytes 2752516
  137.9 77.8 %reduce-scatter.4.cloned.1.call-start = ((), (), s32[]{:S(2)}) async-start(), calls=%async_computation.5 | async-start | bytes 1310720 | tf_op jit(solution)/shard_map/reduce_scatter | solution.py:54
  190.6 55.8 %reduce-scatter.6.cloned.1.call-start = ((), (), s32[]{:S(2)}) async-start(), calls=%async_computation.6 | async-start | bytes 1310720 | tf_op jit(solution)/shard_map/reduce_scatter | solution.py:54
  195.2 20.4 %copy-start.82 = (f32[128]{0:T(128)S(1)}, f32[128]{0:T(128)}, u32[]{:S(2)}) copy-start(f32[128]{0:T(128)} %get-tuple-element.126) | copy-start | bytes 1540
  195.2 21.5 %copy-start.43 = (bf16[2,256,128]{2,1,0:T(8,128)(2,1)S(1)}, bf16[2,256,128]{2,1,0:T(8,128)(2,1)}, u32[]{:S(2)}) copy-start(bf16[2,256,128]{2,1,0:T(8,128)(2,1)} %copy-done.42) | copy-start | bytes 393220
  195.2 21.8 %copy-start.41 = (bf16[2,256,128]{2,1,0:T(8,128)(2,1)S(1)}, bf16[2,256,128]{2,1,0:T(8,128)(2,1)}, u32[]{:S(2)}) copy-start(bf16[2,256,128]{2,1,0:T(8,128)(2,1)} %copy-done.40) | copy-start | bytes 393220
  197.5 19.9 %copy-start.39 = (bf16[2,256,128]{2,1,0:T(8,128)(2,1)S(1)}, bf16[2,256,128]{2,1,0:T(8,128)(2,1)}, u32[]{:S(2)}) copy-start(bf16[2,256,128]{2,1,0:T(8,128)(2,1)} %copy-done.38) | copy-start | bytes 393220
  221.5 55.6 %reduce-scatter.8.cloned.1.call-start = ((), (), s32[]{:S(2)}) async-start(), calls=%async_computation.7 | async-start | bytes 1310720 | tf_op jit(solution)/shard_map/reduce_scatter | solution.py:54
  232.0 14.4 %copy-start.80 = (f32[128]{0:T(128)S(1)}, f32[128]{0:T(128)}, u32[]{:S(2)}) copy-start(f32[128]{0:T(128)} %get-tuple-element.128) | copy-start | bytes 1540
  232.0 15.4 %copy-start.25 = (bf16[2,256,128]{2,1,0:T(8,128)(2,1)S(1)}, bf16[2,256,128]{2,1,0:T(8,128)(2,1)}, u32[]{:S(2)}) copy-start(bf16[2,256,128]{2,1,0:T(8,128)(2,1)} %copy-done.24) | copy-start | bytes 393220
  232.0 15.8 %copy-start.23 = (bf16[2,256,128]{2,1,0:T(8,128)(2,1)S(1)}, bf16[2,256,128]{2,1,0:T(8,128)(2,1)}, u32[]{:S(2)}) copy-start(bf16[2,256,128]{2,1,0:T(8,128)(2,1)} %copy-done.22) | copy-start | bytes 393220
  233.1 15.0 %copy-start.21 = (bf16[2,256,128]{2,1,0:T(8,128)(2,1)S(1)}, bf16[2,256,128]{2,1,0:T(8,128)(2,1)}, u32[]{:S(2)}) copy-start(bf16[2,256,128]{2,1,0:T(8,128)(2,1)} %copy-done.20) | copy-start | bytes 393220
  252.1 723.7 %all-reduce.11.cloned.1.call-start = ((), (), s32[]{:S(2)}) async-start(), calls=%async_computation.8 | async-start | bytes 1835008 | tf_op jit(solution)/shard_map/psum | solution.py:182
  259.4 17.7 %copy-start.44 = (f32[2,16,16,128]{3,2,1,0:T(8,128)S(1)}, f32[2,16,16,128]{3,2,1,0:T(8,128)}, u32[]{:S(2)}) copy-start(f32[2,16,16,128]{3,2,1,0:T(8,128)} %get-tuple-element.133) | copy-start | bytes 786436
  259.4 17.7 %copy-start.78 = (f32[128]{0:T(128)S(1)}, f32[128]{0:T(128)}, u32[]{:S(2)}) copy-start(f32[128]{0:T(128)} %get-tuple-element.130) | copy-start | bytes 1540
  286.9 154.1 %collective-permute-start = (f32[54,256,128]{2,1,0:T(8,128)S(1)}, f32[54,256,128]{2,1,0:T(8,128)}, u32[]{:S(2)}, u32[]{:S(2)}) collective-permute-start(f32[54,256,128]{2,1,0:T(8,128)S(1)} %bitcast.449), channel_id=1, source_target_pairs={{0,4},{4,0},{8,12},{12,8},{16,20},{20,16},{24,28},{28,24},{1,5},{5... | collective-permute-start | bytes 21233672 | tf_op jit(solution)/shard_map/ppermute | solution.py:23
  445.2 160.9 %copy-start.6 = (bf16[512,7,64]{0,2,1:T(8,128)(2,1)S(1)}, bf16[512,7,64]{0,2,1:T(8,128)(2,1)}, u32[]{:S(2)}) copy-start(bf16[512,7,64]{0,2,1:T(8,128)(2,1)} %copy-done.5) | copy-start | bytes 1376260
  445.2 153.2 %collective-permute-start.1 = (f32[54,256,128]{2,1,0:T(8,128)S(1)}, f32[54,256,128]{2,1,0:T(8,128)S(1)}, u32[]{:S(2)}, u32[]{:S(2)}) collective-permute-start(f32[54,256,128]{2,1,0:T(8,128)S(1)} %add.336), channel_id=1, source_target_pairs={{0,8},{4,12},{8,0},{12,4},{16,24},{20,28},{24,16},{28,20},{1,9},{5... | collective-permute-start | bytes 21233672 | tf_op jit(solution)/shard_map/ppermute | solution.py:23
  602.4 376.9 %collective-permute-start.2 = (f32[54,256,128]{2,1,0:T(8,128)}, f32[54,256,128]{2,1,0:T(8,128)}, u32[]{:S(2)}, u32[]{:S(2)}) collective-permute-start(f32[54,256,128]{2,1,0:T(8,128)} %add.337), channel_id=1, source_target_pairs={{0,16},{4,20},{8,24},{12,28},{16,0},{20,4},{24,8},{28,12},{1,17},{... | collective-permute-start | bytes 21233672 | tf_op jit(solution)/shard_map/ppermute | solution.py:23
  608.5 333.3 %copy-start.76 = (f32[7,64]{1,0:T(8,128)S(1)}, f32[7,64]{1,0:T(8,128)}, u32[]{:S(2)}) copy-start(f32[7,64]{1,0:T(8,128)} %param.34) | copy-start | bytes 5380
  608.5 333.9 %copy-start.67 = (f32[7,64,21]{1,2,0:T(8,128)S(1)}, f32[7,64,21]{1,2,0:T(8,128)}, u32[]{:S(2)}) copy-start(f32[7,64,21]{1,2,0:T(8,128)} %param.31) | copy-start | bytes 112900
  608.5 333.9 %copy-start.72 = (f32[7,64,21]{1,2,0:T(8,128)S(1)}, f32[7,64,21]{1,2,0:T(8,128)}, u32[]{:S(2)}) copy-start(f32[7,64,21]{1,2,0:T(8,128)} %param.33) | copy-start | bytes 112900
  608.5 367.3 %copy-start.4 = (f32[7,64,512]{2,1,0:T(8,128)S(1)}, f32[7,64,512]{2,1,0:T(8,128)}, u32[]{:S(2)}) copy-start(f32[7,64,512]{2,1,0:T(8,128)} %param.28) | copy-start | bytes 2752516
  608.5 367.3 %copy-start.49 = (f32[7,64,512]{2,1,0:T(8,128)S(1)}, f32[7,64,512]{2,1,0:T(8,128)}, u32[]{:S(2)}) copy-start(f32[7,64,512]{2,1,0:T(8,128)} %param.30) | copy-start | bytes 2752516
  612.2 329.5 %copy-start.84 = (f32[7,64]{1,0:T(8,128)S(1)}, f32[7,64]{1,0:T(8,128)}, u32[]{:S(2)}) copy-start(f32[7,64]{1,0:T(8,128)} %param.36) | copy-start | bytes 5380
  612.2 329.6 %copy-start.85 = (f32[7,64]{1,0:T(8,128)S(1)}, f32[7,64]{1,0:T(8,128)}, u32[]{:S(2)}) copy-start(f32[7,64]{1,0:T(8,128)} %param.35) | copy-start | bytes 5380
  612.2 330.2 %copy-start.73 = (f32[7,64,21]{1,2,0:T(8,128)S(1)}, f32[7,64,21]{1,2,0:T(8,128)}, u32[]{:S(2)}) copy-start(f32[7,64,21]{1,2,0:T(8,128)} %param.32) | copy-start | bytes 112900
  (54 other events, 165.8 us)
Sparse Core Ops, SparseCore 0:
  10.8 69.0 all-gather.1
  138.0 30.8 all-reduce.8
  190.7 24.9 reduce-scatter.3
  221.6 24.7 reduce-scatter.5
  252.3 24.7 reduce-scatter.7
  608.6 367.1 all-reduce.10
